TPU v7x, 256 devices: a whole 4x4x8 slice. The times are simulated.
256 devices in a mesh: dp: 16 (over z, core), expert: 16 (over y, x).
Axes of the slice: x: 4, y: 4, z: 8, core: 2. Of those that a mesh axis runs over, the one named last changes fastest.
Arguments:
- ssm_state: bfloat16 [1024, 16, 4096], P('expert', None, 'dp'), may hold values from -6 to 6
- conv_state: bfloat16 [1024, 3, 4096], P('expert', None, 'dp'), may hold values from -6 to 6
- new_slot: int32 [1024], replicated, may hold values from 0 to 1023, as said below
- conv_input: bfloat16 [1024, 4096], P('expert', 'dp'), may hold values from -6 to 6
- gate_input: bfloat16 [1024, 4096], P('expert', 'dp'), may hold values from -6 to 6
- conv_weight: float32 [4, 4096], P(None, 'dp'), may hold values from -3 to 3
- conv_bias: float32 [4096], P('dp'), may hold values from -3 to 3
- x_proj_weight: bfloat16 [4096, 288], P('dp'), may hold values from -0.09375 to 0.09375
- step_weight: bfloat16 [256, 4096], P(None, 'dp'), may hold values from -0.375 to 0.375
- step_bias: float32 [4096], P('dp'), may hold values from -3 to -0.5
- decay_log: float32 [16, 4096], P(None, 'dp'), may hold values from 0 to 2
- skip_gain: float32 [4096], P('dp'), may hold values from 0.5 to 1.5
- out_proj_weight: bfloat16 [4096, 4096], P('dp', 'expert'), may hold values from -0.09375 to 0.09375
- residual: bfloat16 [1024, 4096], P(None, 'expert'), may hold values from -6 to 6
- norm_gain: float32 [4096], replicated, may hold values from 0.1 to 1.9
- routes: int32 [1024, 2], replicated, may hold values from 0 to 15, all different within a row; in each aligned block of 64 rows (0 to 63, 64 to 127, ...) at most 20 rows name the same one
- gate_weight: float32 [1024, 2], replicated, may hold values from 0.1 to 0.9
- expert_gate: bfloat16 [16, 4096, 7168], P('expert', None, 'dp'), may hold values from -0.09375 to 0.09375
- expert_up: bfloat16 [16, 4096, 7168], P('expert', None, 'dp'), may hold values from -0.09375 to 0.09375
- expert_down: bfloat16 [16, 7168, 4096], P('expert', 'dp'), may hold values from -0.0625 to 0.0625
Outputs:
- ssm_new: bfloat16 [1024, 16, 4096], P('expert', None, 'dp')
- conv_new: bfloat16 [1024, 3, 4096], P('expert', None, 'dp')
- layer_out: bfloat16 [1024, 4096], P(None, 'expert')
Inputs may be any that keep to these rules, and one draw needn't show every extreme that they name: new_slot is a permutation of the 1024 slots; slot s belongs to expert index s // 64. Of the 64 old slots of one expert index, at most 8 get new slots of any one expert index, and exactly 8 those of some expert index; every expert index sends the same multiset of such counts. `routes`: each row names 2 different experts; within each aligned block of 64 rows (the rows of one expert index) no expert is named by more than 20 rows, a bound that some block reaches.
All inputs are finite; a program needn't handle non-finite values.
Results may differ from a plain program's by a relative error of at most 0.012.
Values may be sent and summed in bfloat16 or wider, within the bound.
A program may use at most 128 MiB of HBM per device.

v0:
```python
import jax
import jax.numpy as jnp
from jax import lax
from jax.sharding import PartitionSpec as P


def dp_total(values):
    return lax.psum(values, "dp")


def body(
    ssm_state,
    conv_state,
    new_slot,
    conv_input,
    gate_input,
    conv_weight,
    conv_bias,
    x_proj_weight,
    step_weight,
    step_bias,
    decay_log,
    skip_gain,
    out_proj_weight,
    residual,
    norm_gain,
    routes,
    gate_weight,
    expert_gate,
    expert_up,
    expert_down,
):
    row_count, state_dim, channels = ssm_state.shape
    owners = lax.axis_size("expert")
    own_index = lax.axis_index("expert")
    move_cap = 2 * row_count // owners
    slot_count = owners * move_cap
    my_slots = lax.dynamic_slice_in_dim(new_slot, own_index * row_count, row_count)
    target = my_slots // row_count
    target_hot = (target[:, None] == jnp.arange(owners)[None, :]).astype(jnp.int32)
    earlier = jnp.sum((jnp.cumsum(target_hot, axis=0) - target_hot) * target_hot, axis=1)
    send_slot = target * move_cap + earlier
    send_hot = (jnp.arange(slot_count)[:, None] == send_slot[None, :]).astype(jnp.bfloat16)
    packed_ssm = (
        jnp.dot(send_hot, ssm_state.reshape(row_count, -1), preferred_element_type=jnp.float32)
        .astype(jnp.bfloat16)
        .reshape(owners, move_cap, -1)
    )
    packed_conv = (
        jnp.dot(send_hot, conv_state.reshape(row_count, -1), preferred_element_type=jnp.float32)
        .astype(jnp.bfloat16)
        .reshape(owners, move_cap, -1)
    )
    recv_ssm, recv_conv = (
        lax.all_to_all(packed_ssm, "expert", split_axis=0, concat_axis=0, tiled=True),
        lax.all_to_all(packed_conv, "expert", split_axis=0, concat_axis=0, tiled=True),
    )
    arriving = (new_slot // row_count == own_index).astype(jnp.int32).reshape(owners, row_count)
    arrive_rank = (jnp.cumsum(arriving, axis=1) - arriving).reshape(-1)
    source_ids = jnp.arange(owners * row_count) // row_count
    recv_slot = source_ids * move_cap + arrive_rank
    new_place = new_slot % row_count
    place_rows = (
        (new_place[None, :] == jnp.arange(row_count)[:, None])
        & (arriving.reshape(-1)[None, :] == 1)
    ).astype(jnp.bfloat16)
    place_slots = (recv_slot[:, None] == jnp.arange(slot_count)[None, :]).astype(jnp.bfloat16)
    place_hot = jnp.dot(place_rows, place_slots, preferred_element_type=jnp.float32).astype(
        jnp.bfloat16
    )
    moved_ssm = (
        jnp.dot(place_hot, recv_ssm.reshape(slot_count, -1), preferred_element_type=jnp.float32)
        .astype(jnp.bfloat16)
        .reshape(row_count, state_dim, channels)
    )
    moved_conv = (
        jnp.dot(place_hot, recv_conv.reshape(slot_count, -1), preferred_element_type=jnp.float32)
        .astype(jnp.bfloat16)
        .reshape(row_count, -1, channels)
    )
    window = jnp.concatenate([moved_conv, conv_input[:, None, :]], axis=1)
    conv_new = window[:, 1:, :]
    conv_sum = (
        jnp.sum(window.astype(jnp.float32) * conv_weight[None, :, :], axis=1) + conv_bias[None, :]
    )
    activated = jax.nn.silu(conv_sum).astype(jnp.bfloat16)
    projected = dp_total(jnp.dot(activated, x_proj_weight, preferred_element_type=jnp.float32))
    rank_dim = step_weight.shape[0]
    step_low = projected[:, :rank_dim]
    b_coef = projected[:, rank_dim : rank_dim + state_dim]
    c_coef = projected[:, rank_dim + state_dim :]
    step_norm = (
        step_low * lax.rsqrt(jnp.mean(step_low * step_low, axis=1, keepdims=True) + 1e-06)
    ).astype(jnp.bfloat16)
    step_size = jax.nn.softplus(
        jnp.dot(step_norm, step_weight, preferred_element_type=jnp.float32) + step_bias[None, :]
    )
    act_float = activated.astype(jnp.float32)
    decays = jnp.exp(step_size[:, None, :] * (-jnp.exp(decay_log))[None, :, :])
    states = (
        decays * moved_ssm.astype(jnp.float32)
        + (step_size * act_float)[:, None, :] * b_coef[:, :, None]
    )
    ssm_new = states.astype(jnp.bfloat16)
    gated_out = (
        (jnp.sum(c_coef[:, :, None] * states, axis=1) + skip_gain[None, :] * act_float)
        * jax.nn.silu(gate_input.astype(jnp.float32))
    ).astype(jnp.bfloat16)
    mamba_mix = dp_total(
        jnp.dot(
            lax.all_gather(gated_out, "expert", axis=0, tiled=True),
            out_proj_weight,
            preferred_element_type=jnp.float32,
        )
    )
    stream = (residual.astype(jnp.float32) + mamba_mix).astype(jnp.bfloat16)
    top_count = routes.shape[1]
    width = stream.shape[1]
    capacity = min(row_count, 5 * row_count * top_count // (2 * owners))
    expert_hot = (
        (routes[:, :, None] == jnp.arange(owners)[None, None, :])
        .astype(jnp.int32)
        .reshape(owners, row_count * top_count, owners)
    )
    prior = jnp.sum((jnp.cumsum(expert_hot, axis=1) - expert_hot) * expert_hot, axis=2)
    slot_of = (routes.reshape(owners, row_count * top_count) * capacity + prior).reshape(
        owners, row_count, top_count
    )
    matches = slot_of[:, :, :, None] == jnp.arange(owners * capacity)[None, None, None, :]
    dispatch_hot = (
        jnp.any(matches, axis=2).astype(jnp.bfloat16).reshape(owners, row_count, owners, capacity)
    )
    combine_w = jnp.sum(
        jnp.where(matches, gate_weight.reshape(owners, row_count, top_count)[:, :, :, None], 0.0),
        axis=2,
    ).reshape(owners, row_count, owners, capacity)
    outgoing = jnp.einsum(
        "orec,ord->eocd",
        dispatch_hot,
        stream.reshape(owners, row_count, width),
        preferred_element_type=jnp.float32,
    ).astype(jnp.bfloat16)
    arrived = lax.all_to_all(outgoing, "expert", split_axis=0, concat_axis=3, tiled=True)
    tokens = arrived.reshape(owners * capacity, -1).astype(jnp.float32)
    normed = (
        tokens
        * lax.rsqrt(jnp.mean(tokens * tokens, axis=1, keepdims=True) + 1e-05)
        * norm_gain[None, :]
    ).astype(jnp.bfloat16)
    gate_val = jnp.dot(normed, expert_gate[0], preferred_element_type=jnp.float32)
    up_val = jnp.dot(normed, expert_up[0], preferred_element_type=jnp.float32)
    hidden = (jax.nn.silu(gate_val) * up_val).astype(jnp.bfloat16)
    partial_out = jnp.dot(hidden, expert_down[0], preferred_element_type=jnp.float32).reshape(
        owners, capacity, -1
    )
    summed = dp_total(partial_out)
    returned = lax.all_to_all(
        summed.astype(jnp.bfloat16), "expert", split_axis=2, concat_axis=0, tiled=True
    ).astype(summed.dtype)
    expert_mix = jnp.einsum(
        "orec,eocd->ord",
        combine_w,
        returned.reshape(owners, owners, capacity, width),
        precision=lax.Precision.HIGHEST,
        preferred_element_type=jnp.float32,
    )
    layer_out = (stream.astype(jnp.float32) + expert_mix.reshape(-1, width)).astype(jnp.bfloat16)
    return (ssm_new, conv_new, layer_out)


def solution(mesh):
    in_specs = (
        P("expert", None, "dp"),
        P("expert", None, "dp"),
        P(),
        P("expert", "dp"),
        P("expert", "dp"),
        P(None, "dp"),
        P("dp"),
        P("dp", None),
        P(None, "dp"),
        P("dp"),
        P(None, "dp"),
        P("dp"),
        P("dp", "expert"),
        P(None, "expert"),
        P(),
        P(),
        P(),
        P("expert", None, "dp"),
        P("expert", None, "dp"),
        P("expert", "dp", None),
    )
    out_specs = (P("expert", None, "dp"), P("expert", None, "dp"), P(None, "expert"))
    return jax.shard_map(body, mesh=mesh, in_specs=in_specs, out_specs=out_specs, check_vma=False)
```

profile of v0, /device:TPU:97, one launch (start us, length us, event | category | flops | bytes accessed | tf_op | source)
XLA Modules:
  0.0 587.0 jit_solution(9232045870672755872)
XLA Ops:
  10.9 6.9 %all-to-all-start = ((bf16[16,8,768]{2,1,0:T(8,128)(2,1)}), bf16[16,8,768]{2,1,0:T(8,128)(2,1)S(1)}, u32[]{:S(2)}, u32[]{:S(2)}) async-start(bf16[16,8,768]{2,1,0:T(8,128)(2,1)} %fusion.30), calls=%async_computation | async-start | bytes 393216 | tf_op jit(solution)/shard_map/all_to_all | solution.py:56
  22.7 2.3 all-to-all-done
  25.0 4.4 all-to-all-start.1
  30.9 108.3 %all-reduce.4.cloned.1.call-done = f32[64,288]{1,0:T(8,128)} async-done(((f32[64,288]{1,0:T(8,128)}), f32[64,288]{1,0:T(8,128)}) %all-reduce.4.cloned.1.call-update) | async-done | bytes 73744 | tf_op jit(solution)/shard_map/psum | solution.py:8
  144.2 19.4 %all_gather.3 = bf16[1024,256]{1,0:T(8,128)(2,1)S(1)} all-gather(bf16[64,256]{1,0:T(8,128)(2,1)S(1)} %fusion.46), channel_id=1, replica_groups=mesh['dp'=16,'expert'=16] {'expert'}, dimensions={0}, use_global_device_ids=true | all-gather | bytes 557056 | tf_op jit(solution)/shard_map/all_gather | solution.py:111
  165.7 2.8 select_reduce_fusion.1
  170.6 109.3 %all-reduce.6.cloned.1.call-done = f32[1024,256]{1,0:T(8,128)} async-done(((f32[1024,256]{1,0:T(8,128)}), f32[1024,256]{1,0:T(8,128)}) %all-reduce.6.cloned.1.call-update) | async-done | bytes 1048592 | tf_op jit(solution)/shard_map/psum | solution.py:8
  282.1 3.0 copy.93
  285.1 6.7 %all-to-all-start.2 = ((bf16[16,16,20,256]{3,1,2,0:T(8,128)(2,1)}), bf16[16,16,20,256]{3,1,2,0:T(8,128)(2,1)S(1)}, u32[]{:S(2)}, u32[]{:S(2)}) async-start(bf16[16,16,20,256]{3,1,2,0:T(8,128)(2,1)} %copy.93), calls=%async_computation.2 | async-start | bytes 5242880 | tf_op jit(solution)/shard_map/all_to_all | solution.py:143
  291.8 41.7 %all-to-all-done.2 = bf16[16,16,20,256]{3,1,2,0:T(8,128)(2,1)S(1)} async-done(((bf16[16,16,20,256]{3,1,2,0:T(8,128)(2,1)}), bf16[16,16,20,256]{3,1,2,0:T(8,128)(2,1)S(1)}, u32[]{:S(2)}, u32[]{:S(2)}) %all-to-all-start.2) | async-done | bytes 2621472 | tf_op jit(solution)/shard_map/all_to_all | solution.py:143
  334.9 1.5 copy.94
  338.4 1.5 fusion.9
  340.5 1.5 fusion.27
  342.1 5.9 %fusion.5 = f32[16,20,4096]{2,0,1:T(8,128)} fusion(bf16[1,448,4096]{2,1,0:T(8,128)(2,1)} %param.39, bf16[16,20,448]{2,1,0:T(8,128)(2,1)S(1)} %dot_general.52), kind=kOutput, calls=%fused_computation.9 | convolution fusion | flops 1174405120 | bytes 9199616 | tf_op jit(solution)/shard_map/dot_general | solution.py:153
  348.0 74.7 %all-reduce.7 = bf16[16,20,4096]{2,0,1:T(8,128)(2,1)S(1)} all-reduce(f32[16,20,4096]{2,0,1:T(8,128)} %fusion.5), channel_id=1, replica_groups=mesh['dp'=16,'expert'=16] {'dp'}, use_global_device_ids=true, to_apply=%region_13.14 | all-reduce | flops 1310720 | bytes 7864320 | tf_op jit(solution)/shard_map/psum | solution.py:8
  422.7 14.9 %copy.96 = bf16[16,20,4096]{1,0,2:T(8,128)(2,1)} copy(bf16[16,20,4096]{2,0,1:T(8,128)(2,1)S(1)} %all-reduce.7) | data formatting | bytes 5242880 | tf_op jit(solution)/shard_map/convert_element_type | solution.py:158
  437.6 34.7 %reshape.150 = bf16[16,2,40960]{2,1,0:T(2,128)(2,1)} reshape(bf16[4096,16,20]{2,1,0:T(8,128)(2,1)} %bitcast.85) | data formatting | bytes 5242880
  472.3 4.1 all-to-all-start.3
  476.5 2.0 select_reduce_fusion
  478.5 3.1 copy.90
  482.4 35.1 %all-to-all-done.3 = bf16[16,2,40960]{2,1,0:T(2,128)(2,1)S(1)} async-done(((bf16[16,2,40960]{2,1,0:T(2,128)(2,1)}), bf16[16,2,40960]{2,1,0:T(2,128)(2,1)S(1)}, u32[]{:S(2)}, u32[]{:S(2)}) %all-to-all-start.3) | async-done | bytes 2621472 | tf_op jit(solution)/shard_map/all_to_all | solution.py:157
  517.5 42.4 %reshape.151 = bf16[4096,16,20]{2,1,0:T(8,128)(2,1)} reshape(bf16[16,2,40960]{2,1,0:T(2,128)(2,1)S(1)} %all-to-all-done.3) | data formatting | bytes 5242880
  559.9 14.0 %copy.98 = bf16[16,20,16,256]{3,2,1,0:T(8,128)(2,1)S(1)} copy(bf16[16,20,16,256]{1,0,3,2:T(8,128)(2,1)} %bitcast.86) | data formatting | bytes 5242880 | tf_op jit(solution)/shard_map/all_to_all | solution.py:157
  573.9 5.3 fusion.15
  (92 shorter events, 27.2 us)
Async XLA Ops:
  7.2 22.8 %copy-start = (bf16[256,288]{0,1:T(8,128)(2,1)S(1)}, bf16[256,288]{0,1:T(8,128)(2,1)}, u32[]{:S(2)}) copy-start(bf16[256,288]{0,1:T(8,128)(2,1)} %param.27) | copy-start | bytes 442372
  7.2 15.1 %copy-start.5 = (bf16[64,256]{1,0:T(8,128)(2,1)S(1)}, bf16[64,256]{1,0:T(8,128)(2,1)}, u32[]{:S(2)}) copy-start(bf16[64,256]{1,0:T(8,128)(2,1)} %param.23) | copy-start | bytes 98308
  10.9 18.7 %copy-start.10 = (f32[4,256]{1,0:T(4,128)S(1)}, f32[4,256]{1,0:T(4,128)}, u32[]{:S(2)}) copy-start(f32[4,256]{1,0:T(4,128)} %param.25) | copy-start | bytes 12292
  10.9 19.0 %copy-start.11 = (f32[256]{0:T(256)S(1)}, f32[256]{0:T(256)}, u32[]{:S(2)}) copy-start(f32[256]{0:T(256)} %param.26) | copy-start | bytes 3076
  10.9 14.1 %all-to-all-start = ((bf16[16,8,768]{2,1,0:T(8,128)(2,1)}), bf16[16,8,768]{2,1,0:T(8,128)(2,1)S(1)}, u32[]{:S(2)}, u32[]{:S(2)}) async-start(bf16[16,8,768]{2,1,0:T(8,128)(2,1)} %fusion.30), calls=%async_computation | async-start | bytes 393216 | tf_op jit(solution)/shard_map/all_to_all | solution.py:56
  19.6 11.3 %copy-start.7 = (f32[16,256]{1,0:T(8,128)S(1)}, f32[16,256]{1,0:T(8,128)}, u32[]{:S(2)}) copy-start(f32[16,256]{1,0:T(8,128)} %param.30) | copy-start | bytes 49156
  19.6 121.5 %copy-start.15 = (bf16[256,256]{1,0:T(8,128)(2,1)S(1)}, bf16[256,256]{1,0:T(8,128)(2,1)}, u32[]{:S(2)}) copy-start(bf16[256,256]{1,0:T(8,128)(2,1)} %param.28) | copy-start | bytes 393220
  19.6 121.5 %copy-start.16 = (f32[256]{0:T(256)S(1)}, f32[256]{0:T(256)}, u32[]{:S(2)}) copy-start(f32[256]{0:T(256)} %param.29) | copy-start | bytes 3076
  25.0 117.2 %all-to-all-start.1 = ((bf16[16,8,4096]{2,1,0:T(8,128)(2,1)}), bf16[16,8,4096]{2,1,0:T(8,128)(2,1)S(1)}, u32[]{:S(2)}, u32[]{:S(2)}) async-start(bf16[16,8,4096]{2,1,0:T(8,128)(2,1)} %fusion.3), calls=%async_computation.1 | async-start | bytes 2097152 | tf_op jit(solution)/shard_map/all_to_all | solution.py:55
  29.4 109.9 %all-reduce.4.cloned.1.call-start = ((), (), s32[]{:S(2)}) async-start(), calls=%async_computation.4 | async-start | bytes 196608 | tf_op jit(solution)/shard_map/psum | solution.py:8
  30.8 249.0 %all-reduce.6.cloned.1.call-start = ((), (), s32[]{:S(2)}) async-start(), calls=%async_computation.5 | async-start | bytes 2097152 | tf_op jit(solution)/shard_map/psum | solution.py:8
  142.2 2.0 copy-start.6
  142.2 2.0 copy-start.12
  142.2 21.4 %copy-start.3 = (bf16[256,256]{1,0:T(8,128)(2,1)S(1)}, bf16[256,256]{1,0:T(8,128)(2,1)}, u32[]{:S(2)}) copy-start(bf16[256,256]{1,0:T(8,128)(2,1)} %param.32) | copy-start | bytes 393220
  142.8 22.1 %copy-start.4 = (s32[1024,2]{0,1:T(2,128)S(1)}, s32[1024,2]{0,1:T(2,128)}, u32[]{:S(2)}) copy-start(s32[1024,2]{0,1:T(2,128)} %param.35) | copy-start | bytes 24580
  144.2 135.6 %copy-start.2 = (bf16[1024,256]{1,0:T(8,128)(2,1)S(1)}, bf16[1024,256]{1,0:T(8,128)(2,1)}, u32[]{:S(2)}) copy-start(bf16[1024,256]{1,0:T(8,128)(2,1)} %param.33) | copy-start | bytes 1572868
  285.1 6.7 %copy-start.8 = (f32[4096]{0:T(1024)S(1)}, f32[4096]{0:T(1024)}, u32[]{:S(2)}) copy-start(f32[4096]{0:T(1024)} %param.34) | copy-start | bytes 49156
  285.1 48.4 %all-to-all-start.2 = ((bf16[16,16,20,256]{3,1,2,0:T(8,128)(2,1)}), bf16[16,16,20,256]{3,1,2,0:T(8,128)(2,1)S(1)}, u32[]{:S(2)}, u32[]{:S(2)}) async-start(bf16[16,16,20,256]{3,1,2,0:T(8,128)(2,1)} %copy.93), calls=%async_computation.2 | async-start | bytes 5242880 | tf_op jit(solution)/shard_map/all_to_all | solution.py:143
  336.4 2.0 copy-start.13
  338.4 2.0 copy-start.14
  472.3 4.1 copy-start.9
  472.3 45.2 %all-to-all-start.3 = ((bf16[16,2,40960]{2,1,0:T(2,128)(2,1)}), bf16[16,2,40960]{2,1,0:T(2,128)(2,1)S(1)}, u32[]{:S(2)}, u32[]{:S(2)}) async-start(bf16[16,2,40960]{2,1,0:T(2,128)(2,1)} %reshape.150), calls=%async_computation.3 | async-start | bytes 5242880 | tf_op jit(solution)/shard_map/all_to_all | solution.py:157
  573.9 6.2 %copy-start.1 = (bf16[256,288]{0,1:T(8,128)(2,1)S(1)}, bf16[256,288]{0,1:T(8,128)(2,1)}, u32[]{:S(2)}) copy-start(bf16[256,288]{0,1:T(8,128)(2,1)} %param.27) | copy-start | bytes 442372
Sparse Core Ops, SparseCore 0:
  33.1 106.0 all-reduce.3
  165.1 114.7 all-reduce.5
where the time goes:
time: 588 us; the launch traced here: 587 us
  waiting for transfers between devices  297 us (51%)
  local copies, waits for them, and re-layouts  123 us (21%)
  blocking collectives  94 us (16%)
  starting transfers between devices  22.1 us (4%)
  matrix products  21.5 us (4%)
  other arithmetic  15.4 us (3%)
  between operations  14.5 us (2%)
    psum x2, waiting for transfers between devices, dp_total(): return lax.psum(values, 'dp')  218 us
    unnamed x41, local copies, waits for them, and re-layouts  82.2 us
    psum x1, blocking collectives, dp_total(): return lax.psum(values, 'dp')  74.7 us
    all_to_all x1, waiting for transfers between devices, body(): lax.all_to_all(outgoing, 'expert', split_axis=0, concat_axis=3, tiled=True)  41.7 us
    all_to_all x1, waiting for transfers between devices, body(): lax.all_to_all(summed.astype(jnp.bfloat16), 'expert', split_axis=2, conca...  35.1 us
    all_gather x1, blocking collectives, body(): lax.all_gather(gated_out, 'expert', axis=0, tiled=True)  19.4 us
    convert_element_type x1, local copies, waits for them, and re-layouts, body(): summed.astype(jnp.bfloat16)  14.9 us
    all_to_all x1, local copies, waits for them, and re-layouts, body(): lax.all_to_all(summed.astype(jnp.bfloat16), 'expert', split_axis=2, conca...  14 us
  transfers between devices with their start and end apart: 6, of which 5 were waited for; matrix products, arithmetic and copies ran while one was open for 4% of the time, Pallas kernels for 0%

commit v1 on v0

--- a/solution.py
+++ b/solution.py
@@ -2,6 +2,22 @@
 import jax.numpy as jnp
 from jax import lax
 from jax.sharding import PartitionSpec as P
+
+
+def pairwise_exchange(array, axis, split, join):
+    ways, here = (lax.axis_size(axis), lax.axis_index(axis))
+    width = array.shape[split] // ways
+    dims = list(array.shape)
+    dims[split] = width
+    height = dims[join]
+    dims[join] = height * ways
+    full = jnp.zeros(dims, array.dtype)
+    for mask in range(ways):
+        part = lax.dynamic_slice_in_dim(array, (here ^ mask) * width, width, axis=split)
+        if mask:
+            part = lax.ppermute(part, axis, [(d, d ^ mask) for d in range(ways)])
+        full = lax.dynamic_update_slice_in_dim(full, part, (here ^ mask) * height, axis=join)
+    return full
 
 
 def dp_total(values):
@@ -140,7 +156,7 @@
         stream.reshape(owners, row_count, width),
         preferred_element_type=jnp.float32,
     ).astype(jnp.bfloat16)
-    arrived = lax.all_to_all(outgoing, "expert", split_axis=0, concat_axis=3, tiled=True)
+    arrived = pairwise_exchange(outgoing, "expert", 0, 3)
     tokens = arrived.reshape(owners * capacity, -1).astype(jnp.float32)
     normed = (
         tokens

time: 588 us -> 613 us (1.043); the launches traced: 587 us -> 604 us
  starting transfers between devices: 22.1 us -> 46.6 us
  waiting for transfers between devices: 297 us -> 284 us
    all_to_all x1 -> x0, waiting for transfers between devices: 41.7 us -> none  [body(): lax.all_to_all(outgoing, 'expert', split_axis=0, concat_axis=3, tiled=True)]
    ppermute x0 -> x15, starting transfers between devices: none -> 31 us  [pairwise_exchange(): part = lax.ppermute(part, axis, [(d, d ^ mask) for d in range(ways)])]
    ppermute x0 -> x15, waiting for transfers between devices: none -> 29.9 us  [pairwise_exchange(): part = lax.ppermute(part, axis, [(d, d ^ mask) for d in range(ways)])]
    all_to_all x1 -> x0, starting transfers between devices: 6.67 us -> none  [body(): lax.all_to_all(outgoing, 'expert', split_axis=0, concat_axis=3, tiled=True)]
    unnamed x41 -> x64, local copies, waits for them, and re-layouts: 82.2 us -> 79.8 us
  transfers between devices with their start and end apart: 6 -> 20, of which waited for: 5 -> 12; matrix products, arithmetic and copies ran while one was open for 4% -> 4% of each run, Pallas kernels for 0% -> 0%
where the time goes in v1:
time: 613 us; the launch traced here: 604 us
  waiting for transfers between devices  284 us (46%)
  local copies, waits for them, and re-layouts  122 us (20%)
  blocking collectives  94.1 us (15%)
  starting transfers between devices  46.6 us (8%)
  matrix products  25.8 us (4%)
  other arithmetic  16 us (3%)
  between operations  14.9 us (2%)
    psum x2, waiting for transfers between devices, dp_total(): return lax.psum(values, 'dp')  217 us
    unnamed x64, local copies, waits for them, and re-layouts  79.8 us
    psum x1, blocking collectives, dp_total(): return lax.psum(values, 'dp')  74.7 us
    all_to_all x1, waiting for transfers between devices, body(): lax.all_to_all(summed.astype(jnp.bfloat16), 'expert', split_axis=2, conca...  35.1 us
    ppermute x15, starting transfers between devices, pairwise_exchange(): part = lax.ppermute(part, axis, [(d, d ^ mask) for d in range(ways)])  31 us
    ppermute x15, waiting for transfers between devices, pairwise_exchange(): part = lax.ppermute(part, axis, [(d, d ^ mask) for d in range(ways)])  29.9 us
    all_gather x1, blocking collectives, body(): lax.all_gather(gated_out, 'expert', axis=0, tiled=True)  19.4 us
    convert_element_type x1, local copies, waits for them, and re-layouts, body(): summed.astype(jnp.bfloat16)  14.9 us
  transfers between devices with their start and end apart: 20, of which 12 were waited for; matrix products, arithmetic and copies ran while one was open for 4% of the time, Pallas kernels for 0%

profile of v1, /device:TPU:97, one launch (start us, length us, event | category | flops | bytes accessed | tf_op | source)
XLA Modules:
  0.0 603.8 jit_solution(12375475246392766249)
XLA Ops:
  10.9 6.9 %all-to-all-start = ((bf16[16,8,768]{2,1,0:T(8,128)(2,1)}), bf16[16,8,768]{2,1,0:T(8,128)(2,1)S(1)}, u32[]{:S(2)}, u32[]{:S(2)}) async-start(bf16[16,8,768]{2,1,0:T(8,128)(2,1)} %fusion.30), calls=%async_computation | async-start | bytes 393216 | tf_op jit(solution)/shard_map/all_to_all | solution.py:72
  25.0 4.4 all-to-all-start.1
  30.9 108.3 %all-reduce.4.cloned.1.call-done = f32[64,288]{1,0:T(8,128)} async-done(((f32[64,288]{1,0:T(8,128)}), f32[64,288]{1,0:T(8,128)}) %all-reduce.4.cloned.1.call-update) | async-done | bytes 73744 | tf_op jit(solution)/shard_map/psum | solution.py:24
  144.2 19.4 %all_gather.3 = bf16[1024,256]{1,0:T(8,128)(2,1)S(1)} all-gather(bf16[64,256]{1,0:T(8,128)(2,1)S(1)} %fusion.46), channel_id=1, replica_groups=mesh['dp'=16,'expert'=16] {'expert'}, dimensions={0}, use_global_device_ids=true | all-gather | bytes 557056 | tf_op jit(solution)/shard_map/all_gather | solution.py:127
  171.1 108.6 %all-reduce.6.cloned.1.call-done = f32[1024,256]{1,0:T(8,128)} async-done(((f32[1024,256]{1,0:T(8,128)}), f32[1024,256]{1,0:T(8,128)}) %all-reduce.6.cloned.1.call-update) | async-done | bytes 1048592 | tf_op jit(solution)/shard_map/psum | solution.py:24
  292.2 3.6 collective-permute-start.5
  303.7 4.8 collective-permute-start.9
  310.4 3.6 collective-permute-done.6
  314.0 3.9 collective-permute-start.11
  317.9 11.9 %collective-permute-done.7 = bf16[1,16,20,256]{3,2,0,1:T(8,128)(2,1)S(1)} collective-permute-done((bf16[1,16,20,256]{3,2,0,1:T(8,128)(2,1)S(1)}, bf16[1,16,20,256]{3,2,0,1:T(8,128)(2,1)S(1)}, u32[]{:S(2)}, u32[]{:S(2)}) %collective-permute-start.7) | collective-permute-done | bytes 163872 | tf_op jit(solution)/shard_map/ppermute | solution.py:18
  330.1 4.0 collective-permute-start.13
  334.2 3.2 collective-permute-start.14
  337.5 5.2 collective-permute-done.13
  342.7 5.1 collective-permute-done.14
  352.0 4.5 fusion.9
  358.3 5.9 fusion.5
  364.2 74.7 %all-reduce.7 = bf16[16,20,4096]{2,0,1:T(8,128)(2,1)S(1)} all-reduce(f32[16,20,4096]{2,0,1:T(8,128)} %fusion.5), channel_id=1, replica_groups=mesh['dp'=16,'expert'=16] {'dp'}, use_global_device_ids=true, to_apply=%region_13.14 | all-reduce | flops 1310720 | bytes 7864320 | tf_op jit(solution)/shard_map/psum | solution.py:24
  438.9 14.9 %copy.168 = bf16[16,20,4096]{1,0,2:T(8,128)(2,1)} copy(bf16[16,20,4096]{2,0,1:T(8,128)(2,1)S(1)} %all-reduce.7) | data formatting | bytes 5242880 | tf_op jit(solution)/shard_map/convert_element_type | solution.py:174
  453.9 34.7 %reshape.146 = bf16[16,2,40960]{2,1,0:T(2,128)(2,1)} reshape(bf16[4096,16,20]{2,1,0:T(8,128)(2,1)} %bitcast.138) | data formatting | bytes 5242880
  488.5 4.3 all-to-all-start.2
  498.9 35.1 %all-to-all-done.2 = bf16[16,2,40960]{2,1,0:T(2,128)(2,1)S(1)} async-done(((bf16[16,2,40960]{2,1,0:T(2,128)(2,1)}), bf16[16,2,40960]{2,1,0:T(2,128)(2,1)S(1)}, u32[]{:S(2)}, u32[]{:S(2)}) %all-to-all-start.2) | async-done | bytes 2621472 | tf_op jit(solution)/shard_map/all_to_all | solution.py:173
  534.0 42.4 %reshape.147 = bf16[4096,16,20]{2,1,0:T(8,128)(2,1)} reshape(bf16[16,2,40960]{2,1,0:T(2,128)(2,1)S(1)} %all-to-all-done.2) | data formatting | bytes 5242880
  576.4 14.0 %copy.170 = bf16[16,20,16,256]{3,2,1,0:T(8,128)(2,1)S(1)} copy(bf16[16,20,16,256]{1,0,3,2:T(8,128)(2,1)} %bitcast.139) | data formatting | bytes 5242880 | tf_op jit(solution)/shard_map/all_to_all | solution.py:173
  590.5 5.3 fusion.14
  (159 shorter events, 60.1 us)
Async XLA Ops:
  10.9 14.1 %all-to-all-start = ((bf16[16,8,768]{2,1,0:T(8,128)(2,1)}), bf16[16,8,768]{2,1,0:T(8,128)(2,1)S(1)}, u32[]{:S(2)}, u32[]{:S(2)}) async-start(bf16[16,8,768]{2,1,0:T(8,128)(2,1)} %fusion.30), calls=%async_computation | async-start | bytes 393216 | tf_op jit(solution)/shard_map/all_to_all | solution.py:72
  19.6 121.5 %copy-start.27 = (bf16[256,256]{1,0:T(8,128)(2,1)S(1)}, bf16[256,256]{1,0:T(8,128)(2,1)}, u32[]{:S(2)}) copy-start(bf16[256,256]{1,0:T(8,128)(2,1)} %param.28) | copy-start | bytes 393220
  19.6 121.5 %copy-start.28 = (f32[256]{0:T(256)S(1)}, f32[256]{0:T(256)}, u32[]{:S(2)}) copy-start(f32[256]{0:T(256)} %param.29) | copy-start | bytes 3076
  25.0 117.2 %all-to-all-start.1 = ((bf16[16,8,4096]{2,1,0:T(8,128)(2,1)}), bf16[16,8,4096]{2,1,0:T(8,128)(2,1)S(1)}, u32[]{:S(2)}, u32[]{:S(2)}) async-start(bf16[16,8,4096]{2,1,0:T(8,128)(2,1)} %fusion.3), calls=%async_computation.1 | async-start | bytes 2097152 | tf_op jit(solution)/shard_map/all_to_all | solution.py:71
  29.4 109.9 %all-reduce.4.cloned.1.call-start = ((), (), s32[]{:S(2)}) async-start(), calls=%async_computation.3 | async-start | bytes 196608 | tf_op jit(solution)/shard_map/psum | solution.py:24
  30.8 248.9 %all-reduce.6.cloned.1.call-start = ((), (), s32[]{:S(2)}) async-start(), calls=%async_computation.4 | async-start | bytes 2097152 | tf_op jit(solution)/shard_map/psum | solution.py:24
  144.2 135.5 %copy-start.5 = (bf16[1024,256]{1,0:T(8,128)(2,1)S(1)}, bf16[1024,256]{1,0:T(8,128)(2,1)}, u32[]{:S(2)}) copy-start(bf16[1024,256]{1,0:T(8,128)(2,1)} %param.33) | copy-start | bytes 1572868
  285.0 7.2 %collective-permute-start = (bf16[1,16,20,256]{3,2,0,1:T(8,128)(2,1)}, bf16[1,16,20,256]{3,2,0,1:T(8,128)(2,1)}, u32[]{:S(2)}, u32[]{:S(2)}) collective-permute-start(bf16[1,16,20,256]{3,2,0,1:T(8,128)(2,1)} %get-tuple-element.34), channel_id=1, source_target_pairs={{0,1},{1,0},{2,3},{3,2},{4,5},{5,4},{6,7},{7,6},{8,9},{9,8},{10,11... | collective-permute-start | bytes 491528 | tf_op jit(solution)/shard_map/ppermute | solution.py:18
  286.3 12.2 %collective-permute-start.1 = (bf16[1,16,20,256]{3,2,0,1:T(8,128)(2,1)}, bf16[1,16,20,256]{3,2,0,1:T(8,128)(2,1)S(1)}, u32[]{:S(2)}, u32[]{:S(2)}) collective-permute-start(bf16[1,16,20,256]{3,2,0,1:T(8,128)(2,1)} %get-tuple-element.33), channel_id=1, source_target_pairs={{0,2},{1,3},{2,0},{3,1},{4,6},{5,7},{6,4},{7,5},{8,10},{9,11},{10,... | collective-permute-start | bytes 491528 | tf_op jit(solution)/shard_map/ppermute | solution.py:18
  288.8 12.0 %collective-permute-start.2 = (bf16[1,16,20,256]{3,2,0,1:T(8,128)(2,1)}, bf16[1,16,20,256]{3,2,0,1:T(8,128)(2,1)S(1)}, u32[]{:S(2)}, u32[]{:S(2)}) collective-permute-start(bf16[1,16,20,256]{3,2,0,1:T(8,128)(2,1)} %get-tuple-element.32), channel_id=1, source_target_pairs={{0,3},{1,2},{2,1},{3,0},{4,7},{5,6},{6,5},{7,4},{8,11},{9,10},{10,... | collective-permute-start | bytes 491528 | tf_op jit(solution)/shard_map/ppermute | solution.py:18
  289.0 14.5 %collective-permute-start.3 = (bf16[1,16,20,256]{3,2,0,1:T(8,128)(2,1)}, bf16[1,16,20,256]{3,2,0,1:T(8,128)(2,1)S(1)}, u32[]{:S(2)}, u32[]{:S(2)}) collective-permute-start(bf16[1,16,20,256]{3,2,0,1:T(8,128)(2,1)} %get-tuple-element.31), channel_id=1, source_target_pairs={{0,4},{1,5},{2,6},{3,7},{4,0},{5,1},{6,2},{7,3},{8,12},{9,13},{10,... | collective-permute-start | bytes 491528 | tf_op jit(solution)/shard_map/ppermute | solution.py:18
  290.5 43.7 %copy-start.6 = (bf16[1,16,20,256]{3,2,0,1:T(8,128)(2,1)S(1)}, bf16[1,16,20,256]{3,2,0,1:T(8,128)(2,1)}, u32[]{:S(2)}) copy-start(bf16[1,16,20,256]{3,2,0,1:T(8,128)(2,1)} %get-tuple-element.20) | copy-start | bytes 491524
  290.5 13.2 %collective-permute-start.4 = (bf16[1,16,20,256]{3,2,0,1:T(8,128)(2,1)}, bf16[1,16,20,256]{3,2,0,1:T(8,128)(2,1)S(1)}, u32[]{:S(2)}, u32[]{:S(2)}) collective-permute-start(bf16[1,16,20,256]{3,2,0,1:T(8,128)(2,1)} %get-tuple-element.30), channel_id=1, source_target_pairs={{0,5},{1,4},{2,7},{3,6},{4,1},{5,0},{6,3},{7,2},{8,13},{9,12},{10,... | collective-permute-start | bytes 491528 | tf_op jit(solution)/shard_map/ppermute | solution.py:18
  292.2 16.3 %collective-permute-start.5 = (bf16[1,16,20,256]{3,2,0,1:T(8,128)(2,1)S(1)}, bf16[1,16,20,256]{3,2,0,1:T(8,128)(2,1)S(1)}, u32[]{:S(2)}, u32[]{:S(2)}) collective-permute-start(bf16[1,16,20,256]{3,2,0,1:T(8,128)(2,1)S(1)} %copy-done.15), channel_id=1, source_target_pairs={{0,6},{1,7},{2,4},{3,5},{4,2},{5,3},{6,0},{7,1},{8,14},{9,15},{10,... | collective-permute-start | bytes 491528 | tf_op jit(solution)/shard_map/ppermute | solution.py:18
  298.5 15.5 %collective-permute-start.6 = (bf16[1,16,20,256]{3,2,0,1:T(8,128)(2,1)S(1)}, bf16[1,16,20,256]{3,2,0,1:T(8,128)(2,1)S(1)}, u32[]{:S(2)}, u32[]{:S(2)}) collective-permute-start(bf16[1,16,20,256]{3,2,0,1:T(8,128)(2,1)S(1)} %copy-done.14), channel_id=1, source_target_pairs={{0,7},{1,6},{2,5},{3,4},{4,3},{5,2},{6,1},{7,0},{8,15},{9,14},{10,... | collective-permute-start | bytes 491528 | tf_op jit(solution)/shard_map/ppermute | solution.py:18
  300.7 29.1 %collective-permute-start.7 = (bf16[1,16,20,256]{3,2,0,1:T(8,128)(2,1)S(1)}, bf16[1,16,20,256]{3,2,0,1:T(8,128)(2,1)S(1)}, u32[]{:S(2)}, u32[]{:S(2)}) collective-permute-start(bf16[1,16,20,256]{3,2,0,1:T(8,128)(2,1)S(1)} %copy-done.13), channel_id=1, source_target_pairs={{0,8},{1,9},{2,10},{3,11},{4,12},{5,13},{6,14},{7,15},{8,0},{9,1},... | collective-permute-start | bytes 491528 | tf_op jit(solution)/shard_map/ppermute | solution.py:18
  303.5 26.6 %collective-permute-start.8 = (bf16[1,16,20,256]{3,2,0,1:T(8,128)(2,1)S(1)}, bf16[1,16,20,256]{3,2,0,1:T(8,128)(2,1)S(1)}, u32[]{:S(2)}, u32[]{:S(2)}) collective-permute-start(bf16[1,16,20,256]{3,2,0,1:T(8,128)(2,1)S(1)} %copy-done.12), channel_id=1, source_target_pairs={{0,9},{1,8},{2,11},{3,10},{4,13},{5,12},{6,15},{7,14},{8,1},{9,0},... | collective-permute-start | bytes 491528 | tf_op jit(solution)/shard_map/ppermute | solution.py:18
  303.7 30.5 %collective-permute-start.9 = (bf16[1,16,20,256]{3,2,0,1:T(8,128)(2,1)S(1)}, bf16[1,16,20,256]{3,2,0,1:T(8,128)(2,1)S(1)}, u32[]{:S(2)}, u32[]{:S(2)}) collective-permute-start(bf16[1,16,20,256]{3,2,0,1:T(8,128)(2,1)S(1)} %copy-done.11), channel_id=1, source_target_pairs={{0,10},{1,11},{2,8},{3,9},{4,14},{5,15},{6,12},{7,13},{8,2},{9,3},... | collective-permute-start | bytes 491528 | tf_op jit(solution)/shard_map/ppermute | solution.py:18
  308.5 28.8 %collective-permute-start.10 = (bf16[1,16,20,256]{3,2,0,1:T(8,128)(2,1)S(1)}, bf16[1,16,20,256]{3,2,0,1:T(8,128)(2,1)S(1)}, u32[]{:S(2)}, u32[]{:S(2)}) collective-permute-start(bf16[1,16,20,256]{3,2,0,1:T(8,128)(2,1)S(1)} %copy-done.10), channel_id=1, source_target_pairs={{0,11},{1,10},{2,9},{3,8},{4,15},{5,14},{6,13},{7,12},{8,3},{9,2},... | collective-permute-start | bytes 491528 | tf_op jit(solution)/shard_map/ppermute | solution.py:18
  314.0 23.4 %collective-permute-start.11 = (bf16[1,16,20,256]{3,2,0,1:T(8,128)(2,1)S(1)}, bf16[1,16,20,256]{3,2,0,1:T(8,128)(2,1)S(1)}, u32[]{:S(2)}, u32[]{:S(2)}) collective-permute-start(bf16[1,16,20,256]{3,2,0,1:T(8,128)(2,1)S(1)} %copy-done.9), channel_id=1, source_target_pairs={{0,12},{1,13},{2,14},{3,15},{4,8},{5,9},{6,10},{7,11},{8,4},{9,5},... | collective-permute-start | bytes 491528 | tf_op jit(solution)/shard_map/ppermute | solution.py:18
  329.9 7.6 %collective-permute-start.12 = (bf16[1,16,20,256]{3,2,0,1:T(8,128)(2,1)S(1)}, bf16[1,16,20,256]{3,2,0,1:T(8,128)(2,1)S(1)}, u32[]{:S(2)}, u32[]{:S(2)}) collective-permute-start(bf16[1,16,20,256]{3,2,0,1:T(8,128)(2,1)S(1)} %copy-done.8), channel_id=1, source_target_pairs={{0,13},{1,12},{2,15},{3,14},{4,9},{5,8},{6,11},{7,10},{8,5},{9,4},... | collective-permute-start | bytes 491528 | tf_op jit(solution)/shard_map/ppermute | solution.py:18
  330.1 12.6 %collective-permute-start.13 = (bf16[1,16,20,256]{3,2,0,1:T(8,128)(2,1)S(1)}, bf16[1,16,20,256]{3,2,0,1:T(8,128)(2,1)S(1)}, u32[]{:S(2)}, u32[]{:S(2)}) collective-permute-start(bf16[1,16,20,256]{3,2,0,1:T(8,128)(2,1)S(1)} %copy-done.7), channel_id=1, source_target_pairs={{0,14},{1,15},{2,12},{3,13},{4,10},{5,11},{6,8},{7,9},{8,6},{9,7},... | collective-permute-start | bytes 491528 | tf_op jit(solution)/shard_map/ppermute | solution.py:18
  334.2 13.6 %collective-permute-start.14 = (bf16[1,16,20,256]{3,2,0,1:T(8,128)(2,1)S(1)}, bf16[1,16,20,256]{3,2,0,1:T(8,128)(2,1)S(1)}, u32[]{:S(2)}, u32[]{:S(2)}) collective-permute-start(bf16[1,16,20,256]{3,2,0,1:T(8,128)(2,1)S(1)} %copy-done.6), channel_id=1, source_target_pairs={{0,15},{1,14},{2,13},{3,12},{4,11},{5,10},{6,9},{7,8},{8,7},{9,6},... | collective-permute-start | bytes 491528 | tf_op jit(solution)/shard_map/ppermute | solution.py:18
  488.5 45.5 %all-to-all-start.2 = ((bf16[16,2,40960]{2,1,0:T(2,128)(2,1)}), bf16[16,2,40960]{2,1,0:T(2,128)(2,1)S(1)}, u32[]{:S(2)}, u32[]{:S(2)}) async-start(bf16[16,2,40960]{2,1,0:T(2,128)(2,1)} %reshape.146), calls=%async_computation.2 | async-start | bytes 5242880 | tf_op jit(solution)/shard_map/all_to_all | solution.py:173
  (25 other events, 378.7 us)
Sparse Core Ops, SparseCore 0:
  33.1 106.0 all-reduce.3
  165.0 114.6 all-reduce.5
